TPU v7x, 128 devices: a whole 4x4x4 slice. The times are simulated.
128 devices in a mesh: list: 8 (over z, core), fsdp: 16 (over x, y).
Axes of the slice: x: 4, y: 4, z: 4, core: 2. Of those that a mesh axis runs over, the one named last changes fastest.
Arguments:
- hidden: bfloat16 [2048, 64, 2048], P(('list', 'fsdp')), may hold values from -6 to 6
- norm_gain: float32 [2048], replicated, may hold values from 0.5 to 1.5
- w_qkv: bfloat16 [2048, 1536], P('fsdp'), may hold values from -0.125 to 0.125
- w_out: bfloat16 [1024, 2048], P('fsdp'), may hold values from -0.1875 to 0.1875
- final_gain: float32 [2048], replicated, may hold values from 0.5 to 1.5
- w_score: float32 [2048], replicated, may hold values from -0.125 to 0.125
- prior: float32 [2048], P(('list', 'fsdp')), may hold values from -8 to 400
- labels: int32 [2048], P(('list', 'fsdp')), may hold values from 0 to 3
- lengths: int32 [64], replicated, may hold values from 1 to 48, 2048 in all
Outputs:
- loss: float32 [], replicated
- grad_qkv: float32 [2048, 1536], P('fsdp', 'list')
- grad_out: float32 [1024, 2048], P('fsdp', 'list')
Inputs may be any that keep to these rules, and one draw needn't show every extreme that they name: `lengths`: the longest list holds exactly 48 passages.
All inputs are finite; a program needn't handle non-finite values.
Results may differ from a plain program's by a relative error of at most 0.025.
Values may be sent and summed in bfloat16 or wider, within the bound.
A program may use at most 128 MiB of HBM per device.

v0:
```python
import jax
import jax.numpy as jnp
from jax import lax
from jax.sharding import Mesh
from jax.sharding import PartitionSpec as P

HEADS = 16
KV_HEADS = 4
HEAD_DIM = 64
PASSAGE_LEN = 64
FSDP = ("fsdp_0", "fsdp_1")
LIST_FSDP = ("list_0", "list_1", "fsdp_0", "fsdp_1")
LIST = ("list_0", "list_1")
epsilon = 1e-05
loss_scale = 64.0


def collected_together(value, axis):
    leaves = jax.tree.leaves(value)
    order = sorted(range(len(leaves)), key=lambda k: -leaves[k].size)
    width = (1, *leaves[order[0]].shape)[-1]
    lines = [
        jnp.pad(leaves[k].reshape(-1), (0, -leaves[k].size % width)).reshape(-1, width)
        for k in order
    ]
    both, at, found = (lax.all_gather(jnp.concatenate(lines), axis), 0, {})
    for k, line in zip(order, lines):
        slab = both[:, at : at + len(line)].reshape(len(both), -1)
        found[k] = slab[:, : leaves[k].size].reshape(-1, *leaves[k].shape)
        at += len(line)
    numbers = iter(range(len(leaves)))
    return jax.tree.map(lambda _: found[next(numbers)], value)


def joined_all(value, axes, combine):
    for axis in axes:
        pieces = collected_together(value, axis)
        value = jax.tree.map(lambda part: part[0], pieces)
        for k in range(1, lax.axis_size(axis)):
            value = combine(value, jax.tree.map(lambda part: part[k], pieces))
    return value


def by_axis(value, axes):
    for axis in axes:
        value = lax.psum(value, axis)
    return value


def own_rows(terms, axes):
    so_far = terms.astype(jnp.bfloat16)
    for axis in axes:
        so_far = lax.psum_scatter(so_far, axis, scatter_dimension=0, tiled=True)
    return so_far.astype(jnp.float32)


def joined_along(parts, dim):
    dims = list(parts.shape[1:])
    dims[dim] *= parts.shape[0]
    return jnp.moveaxis(parts, 0, dim).reshape(dims)


def from_everyone(value, axis):
    copies = jnp.broadcast_to(value, (lax.axis_size(axis), *value.shape))
    return lax.all_to_all(copies, axis, split_axis=0, concat_axis=0, tiled=True)


def gathered_copies(value, axis, dim):
    return joined_along(from_everyone(value, axis), dim)


def in_blocks(value, dim, count):
    dims = value.shape
    parts = value.reshape(*dims[:dim], count, dims[dim] // count, *dims[dim + 1 :])
    return jnp.moveaxis(parts, dim, 0)


def sum_packed(arrays, axis, dims):
    count = lax.axis_size(axis)
    parts = [in_blocks(a, dim, count) for a, dim in zip(arrays, dims)]
    lines = jnp.concatenate([b.reshape(count, -1) for b in parts], axis=1)
    width = max(16, -(-lines.shape[1] // 1024) * 8)
    lines = jnp.pad(lines, ((0, 0), (0, width * 128 - lines.shape[1]))).reshape(-1, 128)
    flat, at, gathered = (lax.psum_scatter(lines, axis, tiled=True).reshape(-1), 0, [])
    for b in parts:
        part = b[0]
        gathered.append(flat[at : at + part.size].reshape(part.shape))
        at += part.size
    return tuple(gathered)


def normed(hidden, norm_gain):
    values = hidden.astype(jnp.float32)
    mean_square = jnp.mean(values * values, -1, keepdims=True)
    return (values * lax.rsqrt(mean_square + epsilon) * norm_gain).astype(jnp.bfloat16)


def attend(projected, passages):
    width_q = HEADS * HEAD_DIM
    width_k = KV_HEADS * HEAD_DIM
    ratio = HEADS // KV_HEADS
    query_part = projected[:, :width_q].reshape(passages, PASSAGE_LEN, KV_HEADS, ratio, HEAD_DIM)
    key_part = projected[:, width_q : width_q + width_k].reshape(
        passages, PASSAGE_LEN, KV_HEADS, HEAD_DIM
    )
    value_part = projected[:, width_q + width_k :].reshape(
        passages, PASSAGE_LEN, KV_HEADS, HEAD_DIM
    )
    scores = jnp.einsum(
        "bqgre,bkge->bgrqk", query_part, key_part, preferred_element_type=jnp.float32
    ) * HEAD_DIM ** (-0.5)
    peak = jnp.max(scores, -1, keepdims=True)
    expo = jnp.exp(scores - peak)
    probs = (expo / jnp.sum(expo, -1, keepdims=True)).astype(jnp.bfloat16)
    attended = jnp.einsum(
        "bgrqk,bkge->bqgre", probs, value_part, preferred_element_type=jnp.float32
    ).astype(jnp.bfloat16)
    return (
        query_part,
        key_part,
        value_part,
        probs,
        attended.reshape(passages, PASSAGE_LEN, width_q),
    )


def attend_back(query_part, key_part, value_part, probs, d_attended, passages):
    d_heads = d_attended.reshape(passages, KV_HEADS, HEADS // KV_HEADS, HEAD_DIM)
    d_probs = jnp.einsum("bgre,bkge->bgrk", d_heads, value_part, preferred_element_type=jnp.float32)
    probs_f = probs.astype(jnp.float32)
    inner = jnp.sum(probs_f * d_probs[:, :, :, None, :], -1, keepdims=True)
    d_scores = (probs_f * (d_probs[:, :, :, None, :] - inner) * HEAD_DIM ** (-0.5)).astype(
        jnp.bfloat16
    )
    d_query = jnp.einsum(
        "bgrqk,bkge->bqgre", d_scores, key_part, preferred_element_type=jnp.float32
    ).astype(jnp.bfloat16)
    d_key = jnp.einsum(
        "bgrqk,bqgre->bkge", d_scores, query_part, preferred_element_type=jnp.float32
    ).astype(jnp.bfloat16)
    d_value = jnp.einsum(
        "bgrqk,bgre->bkge", probs, d_heads, preferred_element_type=jnp.float32
    ).astype(jnp.bfloat16)
    rows = passages * PASSAGE_LEN
    return jnp.concatenate(
        [d_query.reshape(rows, -1), d_key.reshape(rows, -1), d_value.reshape(rows, -1)], 1
    )


def combine_stats(first, second):
    peak = jnp.maximum(first[0], second[0])
    total = first[1] * jnp.exp(first[0] - peak) + second[1] * jnp.exp(second[0] - peak)
    return (peak, total, first[2] + second[2])


def local(hidden, norm_gain, w_qkv, w_out, final_gain, w_score, prior, labels, lengths):
    passages = hidden.shape[0]
    width = hidden.shape[2]
    normal_rows = normed(hidden, norm_gain).reshape(passages * PASSAGE_LEN, width)
    full_qkv, full_out = (
        lax.all_gather(w_qkv, FSDP, axis=0, tiled=True),
        lax.all_gather(w_out, FSDP, axis=0, tiled=True),
    )
    projected = jnp.dot(normal_rows, full_qkv, preferred_element_type=jnp.float32).astype(
        jnp.bfloat16
    )
    query_part, key_part, value_part, probs, attended = attend(projected, passages)
    mixed = jnp.dot(
        attended.reshape(passages * PASSAGE_LEN, -1), full_out, preferred_element_type=jnp.float32
    )
    residual = hidden.astype(jnp.float32) + mixed.reshape(passages, PASSAGE_LEN, width)
    pooled = jnp.mean(residual, 1)
    inverse = lax.rsqrt(jnp.mean(pooled * pooled, -1, keepdims=True) + epsilon)
    unit = pooled * inverse
    score = jnp.sum(unit * final_gain * w_score, -1) + prior
    queries = lengths.shape[0]
    position = lax.axis_index(LIST_FSDP) * passages + jnp.arange(passages, dtype=jnp.int32)
    ends = jnp.cumsum(lengths)
    owner = jnp.sum((position[:, None] >= ends[None, :]).astype(jnp.int32), 1)
    member = (owner[:, None] == jnp.arange(queries, dtype=jnp.int32)[None, :]).astype(jnp.float32)
    label_weight = jnp.exp(labels.astype(jnp.float32))
    label_local = jnp.sum(member * label_weight[:, None], 0)
    local_peak = jnp.max(jnp.where(member > 0, score[:, None], -1e30), 0)
    own_peak = jnp.sum(member * local_peak[None, :], 1)
    expo_local = jnp.sum(member * jnp.exp(score - own_peak)[:, None], 0)
    peak, total, label_total = joined_all(
        (local_peak, expo_local, label_local), LIST_FSDP, combine_stats
    )
    log_norm = peak + jnp.log(total)
    log_prob = score - jnp.sum(member * log_norm[None, :], 1)
    target = label_weight / jnp.sum(member * label_total[None, :], 1)
    loss = by_axis(-loss_scale * jnp.sum(target * log_prob), LIST_FSDP)
    d_score = loss_scale * (jnp.exp(log_prob) - target)
    d_unit = d_score[:, None] * w_score[None, :] * final_gain[None, :]
    d_pooled = inverse * (d_unit - unit * jnp.mean(d_unit * unit, -1, keepdims=True))
    d_rows = (d_pooled / PASSAGE_LEN).astype(jnp.bfloat16)
    attn_sum = jnp.sum(attended, 1, dtype=jnp.float32).astype(jnp.bfloat16)
    d_attended = lax.dot_general(
        d_rows, full_out, (((1,), (1,)), ((), ())), preferred_element_type=jnp.float32
    ).astype(jnp.bfloat16)
    d_projected = attend_back(query_part, key_part, value_part, probs, d_attended, passages)
    qkv_part = own_rows(
        lax.dot_general(
            normal_rows, d_projected, (((0,), (0,)), ((), ())), preferred_element_type=jnp.float32
        ),
        FSDP,
    )
    group_sums = lax.all_to_all(attn_sum, FSDP, split_axis=1, concat_axis=0, tiled=True)
    group_rows = gathered_copies(d_rows, FSDP, 0)
    out_part = lax.dot_general(
        group_sums, group_rows, (((0,), (0,)), ((), ())), preferred_element_type=jnp.float32
    )
    grad_qkv, grad_out = tuple(
        (
            part.astype(jnp.float32)
            for part in sum_packed(
                (qkv_part.astype(jnp.bfloat16), out_part.astype(jnp.bfloat16)), LIST, (1, 1)
            )
        )
    )
    return (loss, grad_qkv, grad_out)


def solution(mesh):
    torus = Mesh(mesh.devices.reshape(4, 2, 4, 4), ("list_0", "list_1", "fsdp_0", "fsdp_1"))
    in_specs = (
        P(LIST_FSDP, None, None),
        P(),
        P(FSDP, None),
        P(FSDP, None),
        P(),
        P(),
        P(LIST_FSDP),
        P(LIST_FSDP),
        P(),
    )
    out_specs = (P(), P(FSDP, LIST), P(FSDP, LIST))
    return jax.shard_map(local, mesh=torus, in_specs=in_specs, out_specs=out_specs, check_vma=False)
```

profile of v0, /device:TPU:0, one launch (start us, length us, event | category | flops | bytes accessed | tf_op | source)
XLA Modules:
  0.0 379.6 jit_solution(12760999220482166367)
XLA Ops:
  16.1 57.7 %all-gather.11.cloned.1.call-done = bf16[2048,1536]{1,0:T(8,128)(2,1)} async-done(((bf16[128,1536]{1,0:T(8,128)(2,1)}), bf16[2048,1536]{1,0:T(8,128)(2,1)}) %all-gather.11.cloned.1.call-update) | async-done | bytes 6291472 | tf_op jit(solution)/shard_map/all_gather | solution.py:161
  73.8 10.0 %convolution_convert_fusion.1 = bf16[1024,1536]{1,0:T(8,128)(2,1)S(1)} fusion(bf16[1024,2048]{1,0:T(8,128)(2,1)} %bitcast.332, bf16[2048,1536]{1,0:T(8,128)(2,1)} %all-gather.11.cloned.1.call-done), kind=kOutput, calls=%fused_computation.28 | convolution fusion | flops 6444023808 | bytes 13631488 | tf_op jit(solution)/shard_map/dot_general | solution.py:164
  88.7 4.0 %reshape.844 = bf16[16,64,4,4,64]{4,3,2,1,0:T(4,128)(2,1)} reshape(bf16[1024,1024]{1,0:T(8,128)(2,1)S(1)} %slice.288) | data formatting | bytes 4194304 | tf_op jit(solution)/shard_map/reshape | solution.py:102
  92.7 8.2 %copy.67 = bf16[16,64,4,4,64]{1,4,3,2,0:T(8,128)(2,1)} copy(bf16[16,64,4,4,64]{4,3,2,1,0:T(4,128)(2,1)} %reshape.844) | data formatting | bytes 4194304 | tf_op jit(solution)/shard_map/reshape | solution.py:102
  101.3 8.6 %fusion.92 = (f32[16,4,4,64]{3,2,1,0:T(4,128)S(1)}, f32[16,4,4,64,64]{3,4,2,1,0:T(8,128)}) fusion(bf16[16,64,4,64,1]{1,3,4,2,0:T(8,128)(2,1)S(1)} %copy-done.3, bf16[16,64,4,4,64]{1,4,3,2,0:T(8,128)(2,1)} %copy.67), kind=kOutput, calls=%fused_computation.172 | convolution fusion | flops 137363520 | bytes 6881280 | tf_op jit(solution)/shard_map/sub | solution.py:113
  109.9 5.7 %convert_reduce_fusion = (bf16[16,4,4,64]{3,2,1,0:T(4,128)(2,1)S(1)}, bf16[16,4,4,64,64]{3,4,2,1,0:T(8,128)(2,1)S(1)}) fusion(f32[16,4,4,64,64]{3,4,2,1,0:T(8,128)} %get-tuple-element.31, f32[16,4,4,64]{3,2,1,0:T(4,128)S(1)} %get-tuple-element.30), kind=kLoop, calls=%fused_computation.2 | loop fusion | flops 4177920 | bytes 6389760 | tf_op jit(solution)/shard_map/bgrqk,bgre->bkge/reduce_sum | solution.py:141
  117.8 5.4 %copy.62 = bf16[16,64,4,4,64]{4,3,2,1,0:T(4,128)(2,1)} copy(bf16[16,64,4,4,64]{4,1,3,2,0:T(8,128)(2,1)S(1)} %get-tuple-element.33) | data formatting | bytes 4194304 | tf_op jit(solution)/shard_map/convert_element_type | solution.py:117
  123.3 7.9 %dot_general.38 = bf16[16,64,1024]{2,1,0:T(8,128)(2,1)} reshape(bf16[16,64,4,4,64]{4,3,2,1,0:T(4,128)(2,1)} %copy.62) | data formatting | bytes 4194304 | tf_op jit(solution)/shard_map/dot_general | solution.py:168
  131.2 8.7 %fusion.6 = f32[16,2048]{1,0:T(8,128)S(1)} fusion(bf16[16,64,2048]{2,1,0:T(8,128)(2,1)} %param.9, bf16[16,64,1024]{2,1,0:T(8,128)(2,1)} %dot_general.38, bf16[1024,2048]{1,0:T(8,128)(2,1)} %all-gather.13.cloned.1.call-done), kind=kOutput, calls=%fused_computation.12 | convolution fusion | flops 4301225984 | bytes 10616832 | tf_op jit(solution)/shard_map/dot_general | solution.py:168
  140.7 11.3 %all-gather.4 = f32[4,3,64]{2,1,0:T(4,128)S(1)} all-gather(f32[1,3,64]{2,1,0:T(4,128)S(1)} %maximum_bitcast_fusion), channel_id=2, replica_groups=mesh['list_0'=4,'list_1'=2,'fsdp_0'=4,'fsdp_1'=4] {'list_0'}, dimensions={0}, use_global_device_ids=true | all-gather | bytes 3840 | tf_op jit(solution)/shard_map/all_gather | solution.py:26
  153.9 11.1 %all-gather.6 = f32[4,3,64]{2,1,0:T(4,128)S(1)} all-gather(f32[1,3,64]{2,1,0:T(4,128)S(1)} %maximum_bitcast_fusion.2), channel_id=4, replica_groups=mesh['list_0'=4,'list_1'=2,'fsdp_0'=4,'fsdp_1'=4] {'fsdp_0'}, dimensions={0}, use_global_device_ids=true | all-gather | bytes 3840 | tf_op jit(solution)/shard_map/all_gather | solution.py:26
  165.1 10.5 %all-gather.7 = f32[4,3,64]{2,1,0:T(4,128)S(1)} all-gather(f32[1,3,64]{2,1,0:T(4,128)S(1)} %maximum_bitcast_fusion.3), channel_id=5, replica_groups=mesh['list_0'=4,'list_1'=2,'fsdp_0'=4,'fsdp_1'=4] {'fsdp_1'}, dimensions={0}, use_global_device_ids=true | all-gather | bytes 3840 | tf_op jit(solution)/shard_map/all_gather | solution.py:26
  178.1 9.1 %convert_bitcast_fusion = bf16[16,64,4,4,64]{1,4,3,2,0:T(8,128)(2,1)} fusion(bf16[16,64,4,64,1]{1,3,4,2,0:T(8,128)(2,1)S(1)} %copy-done.3, bf16[16,4,4,64,64]{3,4,2,1,0:T(8,128)(2,1)} %copy-done, f32[16,4,4,64]{3,2,1,0:T(4,128)S(1)} %fusion.31), kind=kOutput, calls=%fused_computation.24 | convolution fusion | flops 142622784 | bytes 4784128 | tf_op jit(solution)/shard_map/bgrqk,bkge->bqgre/dot_general | solution.py:135
  187.1 10.4 %fusion.28 = bf16[16,64,4,64]{1,3,2,0:T(8,128)(2,1)} fusion(bf16[16,64,4,4,64]{1,4,3,2,0:T(8,128)(2,1)} %copy.67, bf16[16,4,4,64,64]{3,4,2,1,0:T(8,128)(2,1)} %copy-done, f32[16,4,4,64]{3,2,1,0:T(4,128)S(1)} %fusion.31), kind=kOutput, calls=%fused_computation.40 | convolution fusion | flops 141836352 | bytes 4784128 | tf_op jit(solution)/shard_map/bgrqk,bqgre->bkge/dot_general | solution.py:138
  197.5 7.6 %copy.66 = bf16[16,64,4,4,64]{1,0,4,3,2:T(8,128)(2,1)} copy(bf16[16,64,4,4,64]{1,4,3,2,0:T(8,128)(2,1)} %convert_bitcast_fusion) | data formatting | bytes 4194304 | tf_op jit(solution)/shard_map/convert_element_type | solution.py:137
  205.2 5.5 %reshape.849 = bf16[1024,1024]{0,1:T(8,128)(2,1)S(1)} reshape(bf16[16,64,4,4,64]{1,0,4,3,2:T(8,128)(2,1)} %copy.66) | data formatting | bytes 4194304 | tf_op jit(solution)/shard_map/reshape | solution.py:146
  216.8 11.7 %convolution_convert_fusion = bf16[2048,1536]{1,0:T(8,128)(2,1)} fusion(bf16[1024,2048]{1,0:T(8,128)(2,1)} %bitcast.333, bf16[1024,256]{0,1:T(8,128)(2,1)} %reshape.851, bf16[1024,256]{0,1:T(8,128)(2,1)} %reshape.850, bf16[1024,1024]{0,1:T(8,128)(2,1)S(1)} %reshape.849), kind=kOutput, calls=%fused_computation.20 | convolution fusion | flops 6455033856 | bytes 13631488 | tf_op jit(solution)/shard_map/dot_general | solution.py:203
  228.6 62.7 %reduce-scatter.4.cloned.1.call-done = bf16[512,1536]{1,0:T(8,128)(2,1)} async-done(((bf16[2048,1536]{1,0:T(8,128)(2,1)}), bf16[512,1536]{1,0:T(8,128)(2,1)}) %reduce-scatter.4.cloned.1.call-update) | async-done | bytes 1572880 | tf_op jit(solution)/shard_map/reduce_scatter | solution.py:53
  291.5 12.7 %all_to_all.21 = bf16[16,2,512]{2,1,0:T(2,128)(2,1)S(1)} all-to-all(bf16[16,2,512]{2,1,0:T(2,128)(2,1)S(1)} %reshape.882), channel_id=1, replica_groups=mesh['list_0'=4,'list_1'=2,'fsdp_0'=4,'fsdp_1'=4] {'fsdp_0','fsdp_1'}, dimensions={0} | all-to-all | bytes 65536 | tf_op jit(solution)/shard_map/all_to_all | solution.py:208
  309.1 16.2 %all-to-all-done.1 = bf16[16,16,2048]{2,1,0:T(8,128)(2,1)S(1)} async-done(((bf16[16,16,2048]{2,1,0:T(8,128)(2,1)}), bf16[16,16,2048]{2,1,0:T(8,128)(2,1)S(1)}, u32[]{:S(2)}, u32[]{:S(2)}) %all-to-all-start.1) | async-done | bytes 1048608 | tf_op jit(solution)/shard_map/all_to_all | solution.py:65
  325.7 4.3 %reduce-scatter.6.cloned.1.call-done = bf16[128,1536]{1,0:T(8,128)(2,1)} async-done(((bf16[512,1536]{1,0:T(8,128)(2,1)}), bf16[128,1536]{1,0:T(8,128)(2,1)}) %reduce-scatter.6.cloned.1.call-update) | async-done | bytes 393232 | tf_op jit(solution)/shard_map/reduce_scatter | solution.py:53
  334.5 11.2 %psum.28 = f32[]{:T(128)} all-reduce(f32[]{:T(128)S(6)} %mul_shard_map.3), channel_id=1, replica_groups=mesh['list_0'=4,'list_1'=2,'fsdp_0'=4,'fsdp_1'=4] {'list_0'}, use_global_device_ids=true, to_apply=%region_15.16 | all-reduce | flops 1 | bytes 8 | tf_op jit(solution)/shard_map/psum | solution.py:46
  348.7 11.3 %psum.30 = f32[]{:T(128)} all-reduce(f32[]{:T(128)} %psum.29), channel_id=1, replica_groups=mesh['list_0'=4,'list_1'=2,'fsdp_0'=4,'fsdp_1'=4] {'fsdp_0'}, use_global_device_ids=true, to_apply=%region_17.18 | all-reduce | flops 1 | bytes 8 | tf_op jit(solution)/shard_map/psum | solution.py:46
  360.0 9.8 %psum.31 = f32[]{:T(128)} all-reduce(f32[]{:T(128)} %psum.30), channel_id=1, replica_groups=mesh['list_0'=4,'list_1'=2,'fsdp_0'=4,'fsdp_1'=4] {'fsdp_1'}, use_global_device_ids=true, to_apply=%region_18.19 | all-reduce | flops 1 | bytes 8 | tf_op jit(solution)/shard_map/psum | solution.py:46
  (99 shorter events, 43.0 us)
Async XLA Ops:
  7.2 5.9 %copy-start.7 = (f32[2048]{0:T(1024)S(1)}, f32[2048]{0:T(1024)}, u32[]{:S(2)}) copy-start(f32[2048]{0:T(1024)} %param.10) | copy-start | bytes 24580
  7.2 66.7 %all-gather.11.cloned.1.call-start = ((), (), s32[]{:S(2)}) async-start(), calls=%async_computation.5 | async-start | bytes 6684672 | tf_op jit(solution)/shard_map/all_gather | solution.py:161
  7.9 123.3 %all-gather.13.cloned.1.call-start = ((), (), s32[]{:S(2)}) async-start(), calls=%async_computation.6 | async-start | bytes 4456448 | tf_op jit(solution)/shard_map/all_gather | solution.py:162
  8.7 282.6 %reduce-scatter.4.cloned.1.call-start = ((), (), s32[]{:S(2)}) async-start(), calls=%async_computation.7 | async-start | bytes 7864320 | tf_op jit(solution)/shard_map/reduce_scatter | solution.py:53
  9.7 3.5 copy-start.1
  92.7 8.2 %copy-start.4 = (bf16[1024,256]{1,0:T(8,128)(2,1)S(1)}, bf16[1024,256]{1,0:T(8,128)(2,1)}, u32[]{:S(2)}) copy-start(bf16[1024,256]{1,0:T(8,128)(2,1)} %get-tuple-element.26) | copy-start | bytes 1572868
  92.7 8.7 %copy-start.3 = (bf16[16,64,4,64,1]{1,3,4,2,0:T(8,128)(2,1)S(1)}, bf16[16,64,4,64,1]{1,3,4,2,0:T(8,128)(2,1)}, u32[]{:S(2)}) copy-start(bf16[16,64,4,64,1]{1,3,4,2,0:T(8,128)(2,1)} %copy.78) | copy-start | bytes 1572868
  115.7 2.2 copy-start
  131.1 8.9 %copy-start.5 = (f32[2048]{0:T(1024)S(1)}, f32[2048]{0:T(1024)}, u32[]{:S(2)}) copy-start(f32[2048]{0:T(1024)} %param.14) | copy-start | bytes 24580
  131.1 8.9 %copy-start.6 = (f32[2048]{0:T(1024)S(1)}, f32[2048]{0:T(1024)}, u32[]{:S(2)}) copy-start(f32[2048]{0:T(1024)} %param.13) | copy-start | bytes 24580
  131.1 9.1 %copy-start.9 = (f32[16]{0:T(128)S(1)}, f32[16]{0:T(128)}, u32[]{:S(2)}) copy-start(f32[16]{0:T(128)} %param.15) | copy-start | bytes 196
  131.1 9.4 %copy-start.8 = (s32[16]{0:T(128)S(1)}, s32[16]{0:T(128)}, u32[]{:S(2)}) copy-start(s32[16]{0:T(128)} %param.16) | copy-start | bytes 196
  131.2 44.9 %copy-start.2 = (bf16[1024,2048]{1,0:T(8,128)(2,1)S(1)}, bf16[1024,2048]{1,0:T(8,128)(2,1)}, u32[]{:S(2)}) copy-start(bf16[1024,2048]{1,0:T(8,128)(2,1)} %all-gather.13.cloned.1.call-done) | copy-start | bytes 12582916
  228.5 101.5 %reduce-scatter.6.cloned.1.call-start = ((), (), s32[]{:S(2)}) async-start(), calls=%async_computation.8 | async-start | bytes 1966080 | tf_op jit(solution)/shard_map/reduce_scatter | solution.py:53
  305.3 20.1 %all-to-all-start.1 = ((bf16[16,16,2048]{2,1,0:T(8,128)(2,1)}), bf16[16,16,2048]{2,1,0:T(8,128)(2,1)S(1)}, u32[]{:S(2)}, u32[]{:S(2)}) async-start(bf16[16,16,2048]{2,1,0:T(8,128)(2,1)} %broadcast_in_dim.12), calls=%async_computation.3 | async-start | bytes 2097152 | tf_op jit(solution)/shard_map/all_to_all | solution.py:65
  308.9 60.9 %reduce-scatter.8.cloned.1.call-start = ((), (), s32[]{:S(2)}) async-start(), calls=%async_computation.9 | async-start | bytes 737280 | tf_op jit(solution)/shard_map/reduce_scatter | solution.py:84
Sparse Core Ops, SparseCore 0:
  10.2 63.6 all-gather.10
  76.0 50.9 all-gather.12
  228.7 62.6 reduce-scatter.3
  293.6 36.3 reduce-scatter.5
  333.3 31.6 reduce-scatter.7
where the time goes:
time: 386 us; the launch traced here: 380 us
  waiting for transfers between devices  142 us (37%)
  blocking collectives  82.7 us (21%)
  matrix products  63.3 us (16%)
  local copies, waits for them, and re-layouts  56.4 us (15%)
  other arithmetic  15.9 us (4%)
  between operations  15 us (4%)
    reduce_scatter x2, waiting for transfers between devices, own_rows(): so_far = lax.psum_scatter(so_far, axis, scatter_dimension=0, tiled=True)  67 us
    all_gather x1, waiting for transfers between devices, local(): lax.all_gather(w_qkv, FSDP, axis=0, tiled=True)  57.7 us
    psum x4, blocking collectives, by_axis(): value = lax.psum(value, axis)  35.3 us
    all_gather x4, blocking collectives, collected_together(): both, at, found = (lax.all_gather(jnp.concatenate(lines), axis), 0, {})  34.7 us
    all_to_all x1, waiting for transfers between devices, from_everyone(): return lax.all_to_all(copies, axis, split_axis=0, concat_axis=0, tiled=True)  16.2 us
    all_to_all x1, blocking collectives, local(): lax.all_to_all(attn_sum, FSDP, split_axis=1, concat_axis=0, tiled=True)  12.7 us
    reshape x2, local copies, waits for them, and re-layouts, attend(): projected[:, :width_q]  12.2 us
    dot_general x1, matrix products, local(): lax.dot_general(normal_rows, d_projected, (((0,), (0,)), ((), ())), prefe...  11.7 us
  transfers between devices with their start and end apart: 6, of which 4 were waited for; matrix products, arithmetic and copies ran while one was open for 18% of the time, Pallas kernels for 0%

commit v1 on v0

--- a/solution.py
+++ b/solution.py
@@ -158,7 +158,9 @@
     width = hidden.shape[2]
     normal_rows = normed(hidden, norm_gain).reshape(passages * PASSAGE_LEN, width)
     full_qkv, full_out = (
-        lax.all_gather(w_qkv, FSDP, axis=0, tiled=True),
+        jnp.concatenate(
+            lax.all_to_all(jnp.stack([w_qkv] * lax.axis_size(FSDP)), FSDP, 0, 0), axis=0
+        ),
         lax.all_gather(w_out, FSDP, axis=0, tiled=True),
     )
     projected = jnp.dot(normal_rows, full_qkv, preferred_element_type=jnp.float32).astype(

time: 386 us -> 446 us (1.16)
  waiting for transfers between devices: 142 us -> 182 us
  blocking collectives: 82.7 us -> 92.3 us
  starting transfers between devices: 3.85 us -> 11.1 us
    all_to_all x0 -> x1, waiting for transfers between devices: none -> 97.3 us  [local(): lax.all_to_all(jnp.stack([w_qkv] * lax.axis_size(FSDP)), FSDP, 0, 0)]
    all_gather x1 -> x0, waiting for transfers between devices: 57.7 us -> none  [local(): lax.all_gather(w_qkv, FSDP, axis=0, tiled=True)]
    all_gather x4, blocking collectives: 34.7 us -> 44.2 us  [collected_together(): both, at, found = (lax.all_gather(jnp.concatenate(lines), axis), 0, {})]
    all_to_all x0 -> x1, starting transfers between devices: none -> 7.32 us  [local(): lax.all_to_all(jnp.stack([w_qkv] * lax.axis_size(FSDP)), FSDP, 0, 0)]
  transfers between devices with their start and end apart: 6 -> 6, of which waited for: 4 -> 4; matrix products, arithmetic and copies ran while one was open for 18% -> 15% of each run, Pallas kernels for 0% -> 0%
where the time goes in v1:
time: 446 us; the launch traced here: 439 us
  waiting for transfers between devices  182 us (41%)
  blocking collectives  92.3 us (21%)
  matrix products  63.1 us (14%)
  local copies, waits for them, and re-layouts  60 us (13%)
  other arithmetic  15.9 us (4%)
  between operations  15 us (3%)
  starting transfers between devices  11.1 us (2%)
    all_to_all x1, waiting for transfers between devices, local(): lax.all_to_all(jnp.stack([w_qkv] * lax.axis_size(FSDP)), FSDP, 0, 0)  97.3 us
    reduce_scatter x2, waiting for transfers between devices, own_rows(): so_far = lax.psum_scatter(so_far, axis, scatter_dimension=0, tiled=True)  67.1 us
    all_gather x4, blocking collectives, collected_together(): both, at, found = (lax.all_gather(jnp.concatenate(lines), axis), 0, {})  44.2 us
    psum x4, blocking collectives, by_axis(): value = lax.psum(value, axis)  35.3 us
    all_to_all x1, waiting for transfers between devices, from_everyone(): return lax.all_to_all(copies, axis, split_axis=0, concat_axis=0, tiled=True)  16.3 us
    all_to_all x1, blocking collectives, local(): lax.all_to_all(attn_sum, FSDP, split_axis=1, concat_axis=0, tiled=True)  12.7 us
    reshape x2, local copies, waits for them, and re-layouts, attend(): projected[:, :width_q]  12.3 us
    dot_general x1, matrix products, local(): lax.dot_general(normal_rows, d_projected, (((0,), (0,)), ((), ())), prefe...  11.7 us
  transfers between devices with their start and end apart: 6, of which 4 were waited for; matrix products, arithmetic and copies ran while one was open for 15% of the time, Pallas kernels for 0%

profile of v1, /device:TPU:0, one launch (start us, length us, event | category | flops | bytes accessed | tf_op | source)
XLA Modules:
  0.0 438.9 jit_solution(8618489066705550520)
XLA Ops:
  11.4 7.3 %all-to-all-start = ((bf16[16,128,1536]{2,1,0:T(8,128)(2,1)}), bf16[16,128,1536]{2,1,0:T(8,128)(2,1)}, u32[]{:S(2)}, u32[]{:S(2)}) async-start(bf16[16,128,1536]{2,1,0:T(8,128)(2,1)} %stack.2), calls=%async_computation | async-start | bytes 12582912 | tf_op jit(solution)/shard_map/all_to_all | solution.py:162
  26.3 97.3 %all-to-all-done = bf16[16,128,1536]{2,1,0:T(8,128)(2,1)} async-done(((bf16[16,128,1536]{2,1,0:T(8,128)(2,1)}), bf16[16,128,1536]{2,1,0:T(8,128)(2,1)}, u32[]{:S(2)}, u32[]{:S(2)}) %all-to-all-start) | async-done | bytes 6291488 | tf_op jit(solution)/shard_map/all_to_all | solution.py:162
  123.6 10.1 %convolution_convert_fusion.1 = bf16[1024,1536]{1,0:T(8,128)(2,1)S(1)} fusion(bf16[1024,2048]{1,0:T(8,128)(2,1)} %bitcast.333, bf16[2048,1536]{1,0:T(8,128)(2,1)} %bitcast.2), kind=kOutput, calls=%fused_computation.28 | convolution fusion | flops 6444023808 | bytes 13631488 | tf_op jit(solution)/shard_map/dot_general | solution.py:166
  142.5 8.3 %copy.67 = bf16[16,64,4,4,64]{1,4,3,2,0:T(8,128)(2,1)} copy(bf16[16,64,4,4,64]{4,3,2,1,0:T(4,128)(2,1)} %reshape.850) | data formatting | bytes 4194304 | tf_op jit(solution)/shard_map/reshape | solution.py:102
  151.2 8.6 %fusion.92 = (f32[16,4,4,64]{3,2,1,0:T(4,128)S(1)}, f32[16,4,4,64,64]{3,4,2,1,0:T(8,128)}) fusion(bf16[16,64,4,64,1]{1,3,4,2,0:T(8,128)(2,1)S(1)} %copy-done.3, bf16[16,64,4,4,64]{1,4,3,2,0:T(8,128)(2,1)} %copy.67), kind=kOutput, calls=%fused_computation.172 | convolution fusion | flops 137363520 | bytes 6881280 | tf_op jit(solution)/shard_map/sub | solution.py:113
  159.8 5.7 %convert_reduce_fusion = (bf16[16,4,4,64]{3,2,1,0:T(4,128)(2,1)S(1)}, bf16[16,4,4,64,64]{3,4,2,1,0:T(8,128)(2,1)S(1)}) fusion(f32[16,4,4,64,64]{3,4,2,1,0:T(8,128)} %get-tuple-element.31, f32[16,4,4,64]{3,2,1,0:T(4,128)S(1)} %get-tuple-element.30), kind=kLoop, calls=%fused_computation.2 | loop fusion | flops 4177920 | bytes 6389760 | tf_op jit(solution)/shard_map/bgrqk,bgre->bkge/reduce_sum | solution.py:141
  167.7 5.4 %copy.62 = bf16[16,64,4,4,64]{4,3,2,1,0:T(4,128)(2,1)} copy(bf16[16,64,4,4,64]{4,1,3,2,0:T(8,128)(2,1)S(1)} %get-tuple-element.33) | data formatting | bytes 4194304 | tf_op jit(solution)/shard_map/convert_element_type | solution.py:117
  173.1 7.9 %dot_general.38 = bf16[16,64,1024]{2,1,0:T(8,128)(2,1)} reshape(bf16[16,64,4,4,64]{4,3,2,1,0:T(4,128)(2,1)} %copy.62) | data formatting | bytes 4194304 | tf_op jit(solution)/shard_map/dot_general | solution.py:170
  181.0 8.7 %fusion.6 = f32[16,2048]{1,0:T(8,128)S(1)} fusion(bf16[16,64,2048]{2,1,0:T(8,128)(2,1)} %param.9, bf16[16,64,1024]{2,1,0:T(8,128)(2,1)} %dot_general.38, bf16[1024,2048]{1,0:T(8,128)(2,1)} %all-gather.10.cloned.1.call-done), kind=kOutput, calls=%fused_computation.12 | convolution fusion | flops 4301225984 | bytes 10616832 | tf_op jit(solution)/shard_map/dot_general | solution.py:170
  190.5 15.0 %all-gather.4 = f32[4,3,64]{2,1,0:T(4,128)S(1)} all-gather(f32[1,3,64]{2,1,0:T(4,128)S(1)} %maximum_bitcast_fusion), channel_id=2, replica_groups=mesh['list_0'=4,'list_1'=2,'fsdp_0'=4,'fsdp_1'=4] {'list_0'}, dimensions={0}, use_global_device_ids=true | all-gather | bytes 3840 | tf_op jit(solution)/shard_map/all_gather | solution.py:26
  207.4 12.8 %all-gather.6 = f32[4,3,64]{2,1,0:T(4,128)S(1)} all-gather(f32[1,3,64]{2,1,0:T(4,128)S(1)} %maximum_bitcast_fusion.2), channel_id=4, replica_groups=mesh['list_0'=4,'list_1'=2,'fsdp_0'=4,'fsdp_1'=4] {'fsdp_0'}, dimensions={0}, use_global_device_ids=true | all-gather | bytes 3840 | tf_op jit(solution)/shard_map/all_gather | solution.py:26
  220.3 14.6 %all-gather.7 = f32[4,3,64]{2,1,0:T(4,128)S(1)} all-gather(f32[1,3,64]{2,1,0:T(4,128)S(1)} %maximum_bitcast_fusion.3), channel_id=5, replica_groups=mesh['list_0'=4,'list_1'=2,'fsdp_0'=4,'fsdp_1'=4] {'fsdp_1'}, dimensions={0}, use_global_device_ids=true | all-gather | bytes 3840 | tf_op jit(solution)/shard_map/all_gather | solution.py:26
  237.4 9.1 %convert_bitcast_fusion = bf16[16,64,4,4,64]{1,4,3,2,0:T(8,128)(2,1)} fusion(bf16[16,64,4,64,1]{1,3,4,2,0:T(8,128)(2,1)S(1)} %copy-done.3, bf16[16,4,4,64,64]{3,4,2,1,0:T(8,128)(2,1)} %copy-done, f32[16,4,4,64]{3,2,1,0:T(4,128)S(1)} %fusion.31), kind=kOutput, calls=%fused_computation.24 | convolution fusion | flops 142622784 | bytes 4784128 | tf_op jit(solution)/shard_map/bgrqk,bkge->bqgre/dot_general | solution.py:135
  246.5 10.1 %fusion.28 = bf16[16,64,4,64]{1,3,2,0:T(8,128)(2,1)} fusion(bf16[16,64,4,4,64]{1,4,3,2,0:T(8,128)(2,1)} %copy.67, bf16[16,4,4,64,64]{3,4,2,1,0:T(8,128)(2,1)} %copy-done, f32[16,4,4,64]{3,2,1,0:T(4,128)S(1)} %fusion.31), kind=kOutput, calls=%fused_computation.40 | convolution fusion | flops 141836352 | bytes 4784128 | tf_op jit(solution)/shard_map/bgrqk,bqgre->bkge/dot_general | solution.py:138
  256.6 7.6 %copy.66 = bf16[16,64,4,4,64]{1,0,4,3,2:T(8,128)(2,1)} copy(bf16[16,64,4,4,64]{1,4,3,2,0:T(8,128)(2,1)} %convert_bitcast_fusion) | data formatting | bytes 4194304 | tf_op jit(solution)/shard_map/convert_element_type | solution.py:137
  264.2 5.5 %reshape.855 = bf16[1024,1024]{0,1:T(8,128)(2,1)S(1)} reshape(bf16[16,64,4,4,64]{1,0,4,3,2:T(8,128)(2,1)} %copy.66) | data formatting | bytes 4194304 | tf_op jit(solution)/shard_map/reshape | solution.py:146
  275.9 11.7 %convolution_convert_fusion = bf16[2048,1536]{1,0:T(8,128)(2,1)} fusion(bf16[1024,2048]{1,0:T(8,128)(2,1)} %bitcast.334, bf16[1024,256]{0,1:T(8,128)(2,1)} %reshape.857, bf16[1024,256]{0,1:T(8,128)(2,1)} %reshape.856, bf16[1024,1024]{0,1:T(8,128)(2,1)S(1)} %reshape.855), kind=kOutput, calls=%fused_computation.20 | convolution fusion | flops 6455033856 | bytes 13631488 | tf_op jit(solution)/shard_map/dot_general | solution.py:205
  287.7 62.8 %reduce-scatter.4.cloned.1.call-done = bf16[512,1536]{1,0:T(8,128)(2,1)} async-done(((bf16[2048,1536]{1,0:T(8,128)(2,1)}), bf16[512,1536]{1,0:T(8,128)(2,1)}) %reduce-scatter.4.cloned.1.call-update) | async-done | bytes 1572880 | tf_op jit(solution)/shard_map/reduce_scatter | solution.py:53
  350.6 12.7 %all_to_all.26 = bf16[16,2,512]{2,1,0:T(2,128)(2,1)S(1)} all-to-all(bf16[16,2,512]{2,1,0:T(2,128)(2,1)S(1)} %reshape.888), channel_id=1, replica_groups=mesh['list_0'=4,'list_1'=2,'fsdp_0'=4,'fsdp_1'=4] {'fsdp_0','fsdp_1'}, dimensions={0} | all-to-all | bytes 65536 | tf_op jit(solution)/shard_map/all_to_all | solution.py:210
  368.2 16.3 %all-to-all-done.2 = bf16[16,16,2048]{2,1,0:T(8,128)(2,1)S(1)} async-done(((bf16[16,16,2048]{2,1,0:T(8,128)(2,1)}), bf16[16,16,2048]{2,1,0:T(8,128)(2,1)S(1)}, u32[]{:S(2)}, u32[]{:S(2)}) %all-to-all-start.2) | async-done | bytes 1048608 | tf_op jit(solution)/shard_map/all_to_all | solution.py:65
  385.0 4.3 reduce-scatter.6.cloned.1.call-done
  393.8 11.2 %psum.28 = f32[]{:T(128)} all-reduce(f32[]{:T(128)S(6)} %mul_shard_map.3), channel_id=1, replica_groups=mesh['list_0'=4,'list_1'=2,'fsdp_0'=4,'fsdp_1'=4] {'list_0'}, use_global_device_ids=true, to_apply=%region_15.16 | all-reduce | flops 1 | bytes 8 | tf_op jit(solution)/shard_map/psum | solution.py:46
  408.1 11.3 %psum.30 = f32[]{:T(128)} all-reduce(f32[]{:T(128)} %psum.29), channel_id=1, replica_groups=mesh['list_0'=4,'list_1'=2,'fsdp_0'=4,'fsdp_1'=4] {'fsdp_0'}, use_global_device_ids=true, to_apply=%region_17.18 | all-reduce | flops 1 | bytes 8 | tf_op jit(solution)/shard_map/psum | solution.py:46
  419.3 9.8 %psum.31 = f32[]{:T(128)} all-reduce(f32[]{:T(128)} %psum.30), channel_id=1, replica_groups=mesh['list_0'=4,'list_1'=2,'fsdp_0'=4,'fsdp_1'=4] {'fsdp_1'}, use_global_device_ids=true, to_apply=%region_18.19 | all-reduce | flops 1 | bytes 8 | tf_op jit(solution)/shard_map/psum | solution.py:46
  (101 shorter events, 49.8 us)
Async XLA Ops:
  11.4 8.1 %copy-start.9 = (s32[64]{0:T(128)S(1)}, s32[64]{0:T(128)}, u32[]{:S(2)}) copy-start(s32[64]{0:T(128)} %param.17) | copy-start | bytes 772
  11.4 112.2 %all-to-all-start = ((bf16[16,128,1536]{2,1,0:T(8,128)(2,1)}), bf16[16,128,1536]{2,1,0:T(8,128)(2,1)}, u32[]{:S(2)}, u32[]{:S(2)}) async-start(bf16[16,128,1536]{2,1,0:T(8,128)(2,1)} %stack.2), calls=%async_computation | async-start | bytes 12582912 | tf_op jit(solution)/shard_map/all_to_all | solution.py:162
  18.8 4.6 %copy-start.7 = (f32[2048]{0:T(1024)S(1)}, f32[2048]{0:T(1024)}, u32[]{:S(2)}) copy-start(f32[2048]{0:T(1024)} %param.10) | copy-start | bytes 24580
  18.8 162.2 %all-gather.10.cloned.1.call-start = ((), (), s32[]{:S(2)}) async-start(), calls=%async_computation.6 | async-start | bytes 4456448 | tf_op jit(solution)/shard_map/all_gather | solution.py:164
  19.5 330.9 %reduce-scatter.4.cloned.1.call-start = ((), (), s32[]{:S(2)}) async-start(), calls=%async_computation.7 | async-start | bytes 7864320 | tf_op jit(solution)/shard_map/reduce_scatter | solution.py:53
  19.9 3.5 copy-start.1
  142.5 8.3 %copy-start.4 = (bf16[1024,256]{1,0:T(8,128)(2,1)S(1)}, bf16[1024,256]{1,0:T(8,128)(2,1)}, u32[]{:S(2)}) copy-start(bf16[1024,256]{1,0:T(8,128)(2,1)} %get-tuple-element.26) | copy-start | bytes 1572868
  142.5 8.7 %copy-start.3 = (bf16[16,64,4,64,1]{1,3,4,2,0:T(8,128)(2,1)S(1)}, bf16[16,64,4,64,1]{1,3,4,2,0:T(8,128)(2,1)}, u32[]{:S(2)}) copy-start(bf16[16,64,4,64,1]{1,3,4,2,0:T(8,128)(2,1)} %copy.78) | copy-start | bytes 1572868
  165.5 2.2 copy-start
  181.0 8.9 %copy-start.5 = (f32[2048]{0:T(1024)S(1)}, f32[2048]{0:T(1024)}, u32[]{:S(2)}) copy-start(f32[2048]{0:T(1024)} %param.14) | copy-start | bytes 24580
  181.0 8.9 %copy-start.6 = (f32[2048]{0:T(1024)S(1)}, f32[2048]{0:T(1024)}, u32[]{:S(2)}) copy-start(f32[2048]{0:T(1024)} %param.13) | copy-start | bytes 24580
  181.0 9.1 %copy-start.10 = (f32[16]{0:T(128)S(1)}, f32[16]{0:T(128)}, u32[]{:S(2)}) copy-start(f32[16]{0:T(128)} %param.15) | copy-start | bytes 196
  181.0 9.4 %copy-start.8 = (s32[16]{0:T(128)S(1)}, s32[16]{0:T(128)}, u32[]{:S(2)}) copy-start(s32[16]{0:T(128)} %param.16) | copy-start | bytes 196
  181.0 54.5 %copy-start.2 = (bf16[1024,2048]{1,0:T(8,128)(2,1)S(1)}, bf16[1024,2048]{1,0:T(8,128)(2,1)}, u32[]{:S(2)}) copy-start(bf16[1024,2048]{1,0:T(8,128)(2,1)} %all-gather.10.cloned.1.call-done) | copy-start | bytes 12582916
  287.6 101.7 %reduce-scatter.6.cloned.1.call-start = ((), (), s32[]{:S(2)}) async-start(), calls=%async_computation.8 | async-start | bytes 1966080 | tf_op jit(solution)/shard_map/reduce_scatter | solution.py:53
  364.4 20.2 %all-to-all-start.2 = ((bf16[16,16,2048]{2,1,0:T(8,128)(2,1)}), bf16[16,16,2048]{2,1,0:T(8,128)(2,1)S(1)}, u32[]{:S(2)}, u32[]{:S(2)}) async-start(bf16[16,16,2048]{2,1,0:T(8,128)(2,1)} %broadcast_in_dim.12), calls=%async_computation.4 | async-start | bytes 2097152 | tf_op jit(solution)/shard_map/all_to_all | solution.py:65
  368.1 61.0 %reduce-scatter.8.cloned.1.call-start = ((), (), s32[]{:S(2)}) async-start(), calls=%async_computation.9 | async-start | bytes 737280 | tf_op jit(solution)/shard_map/reduce_scatter | solution.py:84
Sparse Core Ops, SparseCore 0:
  21.7 119.7 all-gather.9
  287.7 62.6 reduce-scatter.3
  352.9 36.3 reduce-scatter.5
  392.6 31.6 reduce-scatter.7
